TPU v7x, 256 devices: a whole 4x4x8 slice. The times are simulated.
256 devices in a mesh: dp: 32 (over z, y), tensor: 8 (over x, core).
Axes of the slice: x: 4, y: 4, z: 8, core: 2. Of those that a mesh axis runs over, the one named last changes fastest.
Arguments:
- hidden: bfloat16 [4096, 26624], P('dp', 'tensor'), may hold values from -6 to 6
- out_grad: bfloat16 [4096, 8192], P(('dp', 'tensor')), may hold values from -0.375 to 0.375
- master: float32 [8192, 26624], P('dp', 'tensor'), may hold values from -0.3125 to 0.3125
- first_moment: bfloat16 [8192, 26624], P('dp', 'tensor'), may hold values from -4 to 4
- second_moment: bfloat16 [8192, 26624], P('dp', 'tensor'), may hold values from 0.049804688 to 1
- row_counts: int32 [8], replicated, may hold values from 2816 to 3840, as said below
- step_count: int32 [1], replicated, may hold values from 1 to 11
Outputs:
- adam_update: float32 [8192, 26624], P('dp', 'tensor')
- weights_tp: bfloat16 [8192, 30720], P('dp', 'tensor')
Inputs may be any that keep to these rules, and one draw needn't show every extreme that they name: Tensor index j takes row_counts[j] consecutive hidden units in order; they sum to 26624; offsets[j] differs from j * 3328 by at most 256; the largest count equals 3840.
All inputs are finite; a program needn't handle non-finite values.
Results may differ from a plain program's by a relative error of at most 0.0045.
Values may be sent and summed in bfloat16 or wider, within the bound.
No kernel may reach another device: no remote copies, remote signals or barrier semaphores. Data moves between devices by JAX's collectives and lax.ppermute only.
A program may use at most 192 MiB of HBM per device.

v0:
```python
import math
import jax
import jax.numpy as jnp
from jax import lax
from jax.sharding import PartitionSpec as P

DRIFT = 256
CAP = 3840
beta_first = 0.9
beta_second = 0.95
epsilon = 1e-08
decay_rate = 0.1
learn_rate = 0.001


def extended(cells, sides, width):
    for axis, dim in sides:
        count = lax.axis_size(axis)
        ends = count - 1
        head = lax.slice_in_dim(cells, 0, width, axis=dim)
        tail = lax.slice_in_dim(cells, cells.shape[dim] - width, cells.shape[dim], axis=dim)
        cells = jnp.concatenate(
            [
                lax.ppermute(tail, axis, [(i, (i + 1) % count) for i in range(ends)]),
                cells,
                lax.ppermute(head, axis, [((i + 1) % count, i) for i in range(ends)]),
            ],
            axis=dim,
        )
    return cells


def adamw(gradient, master, first_moment, second_moment, steps_done):
    first_new = beta_first * first_moment + (1.0 - beta_first) * gradient
    second_new = beta_second * second_moment + (1.0 - beta_second) * gradient * gradient
    first_fix = 1.0 - jnp.power(beta_first, steps_done)
    second_fix = 1.0 - jnp.power(beta_second, steps_done)
    update = (
        first_new / first_fix / (jnp.sqrt(second_new / second_fix) + epsilon) + decay_rate * master
    )
    master_new = master - learn_rate * update
    return (master_new, update)


def relayout(weights, row_counts):
    shard_rows = weights.shape[0]
    shard_width = weights.shape[1]
    offsets = jnp.cumsum(row_counts) - row_counts
    position = lax.axis_index("tensor")
    first_slot = lax.dynamic_index_in_dim(offsets, position, keepdims=False)
    length = lax.dynamic_index_in_dim(row_counts, position, keepdims=False)
    padded = extended(weights, (("tensor", 1),), DRIFT)
    widened = jnp.concatenate([padded, jnp.zeros((shard_rows, 2 * DRIFT), jnp.bfloat16)], axis=1)
    start = first_slot - position * shard_width + DRIFT
    window = lax.dynamic_slice_in_dim(widened, start, CAP, 1)
    slot_index = jnp.arange(CAP, dtype=jnp.int32)
    return jnp.where((slot_index < length)[None, :], window, jnp.zeros((), jnp.bfloat16))


def per_device(hidden, out_grad, master, first_moment, second_moment, row_counts, step_count):
    shard_rows = master.shape[0]
    hidden_units = hidden.shape[1]
    regrouped = lax.all_to_all(out_grad, "dp", split_axis=1, concat_axis=0, tiled=True)
    spread = lax.all_gather(regrouped, "tensor", axis=0, tiled=True)
    tensor_count = lax.axis_size("tensor")
    data_count = lax.axis_size("dp")
    local_tokens = out_grad.shape[0]
    group_tokens = hidden.shape[0]
    owned_cols = spread.reshape(tensor_count, data_count, local_tokens, shard_rows)
    shard_piece = lax.all_gather(hidden, "dp", axis=0, tiled=True)
    groups = shard_piece.shape[0] // group_tokens
    per_turn = math.gcd(groups, 4)
    turns = groups // per_turn
    activations = shard_piece.reshape(groups, tensor_count, local_tokens, hidden_units)

    def one_turn(turn_index, running):
        grad_block = lax.dynamic_slice_in_dim(owned_cols, turn_index * per_turn, per_turn, 1)
        act_block = lax.dynamic_slice_in_dim(activations, turn_index * per_turn, per_turn, 0)
        partial_value = jnp.einsum(
            "tgrd,gtrf->gdf", grad_block, act_block, preferred_element_type=jnp.float32
        )
        rounded = lax.optimization_barrier(partial_value.astype(jnp.bfloat16)).astype(jnp.float32)
        return running + jnp.sum(rounded, axis=0)

    gradient = lax.fori_loop(0, turns, one_turn, jnp.zeros((shard_rows, hidden_units), jnp.float32))
    steps_done = step_count[0].astype(jnp.float32)
    master_new, update = adamw(
        gradient,
        master,
        first_moment.astype(jnp.float32),
        second_moment.astype(jnp.float32),
        steps_done,
    )
    laid = relayout(master_new.astype(jnp.bfloat16), row_counts)
    outputs = [(update, laid)]
    joined = [jnp.concatenate([entry[slot] for entry in outputs], axis=0) for slot in range(2)]
    return (joined[0], joined[1])


def solution(mesh):
    return jax.shard_map(
        per_device,
        mesh=mesh,
        in_specs=(
            P("dp", "tensor"),
            P(("dp", "tensor"), None),
            P("dp", "tensor"),
            P("dp", "tensor"),
            P("dp", "tensor"),
            P(),
            P(),
        ),
        out_specs=(P("dp", "tensor"), P("dp", "tensor")),
        check_vma=False,
    )
```

profile of v0, /device:TPU:1, one launch (start us, length us, event | category | flops | bytes accessed | tf_op | source)
XLA Modules:
  0.0 353.1 jit_solution(3971043392902554566)
XLA Ops:
  7.2 0.0 all-gather.3.cloned.1.call-start
  7.2 1.0 copy.20
  8.2 23.1 %all_to_all.19 = bf16[16,32,256]{2,0,1:T(8,128)(2,1)} all-to-all(bf16[16,32,256]{2,0,1:T(8,128)(2,1)S(1)} %bitcast.22), channel_id=1, replica_groups=mesh['dp'=32,'tensor'=8] {'dp'}, dimensions={1} | all-to-all | bytes 524288 | tf_op jit(solution)/shard_map/all_to_all | solution.py:63
  31.3 0.0 all-gather.3.cloned.1.call-update
  31.3 0.0 all-gather.5.cloned.1.call-start
  31.4 0.7 all-gather.5.cloned.1.call-update
  32.8 0.8 reduce-window.9
  33.7 1.2 dynamic_slice.24
  34.9 0.7 bitcast_subtract_fusion
  35.6 21.4 %all-gather.3.cloned.1.call-done = bf16[4096,256]{1,0:T(8,128)(2,1)} async-done(((bf16[512,256]{1,0:T(8,128)(2,1)}), bf16[4096,256]{1,0:T(8,128)(2,1)}) %all-gather.3.cloned.1.call-update) | async-done | bytes 2097168 | tf_op jit(solution)/shard_map/all_gather | solution.py:64
  56.9 198.3 %all-gather.5.cloned.1.call-done = bf16[4096,3328]{1,0:T(8,128)(2,1)} async-done(((bf16[128,3328]{1,0:T(8,128)(2,1)}), bf16[4096,3328]{1,0:T(8,128)(2,1)}) %all-gather.5.cloned.1.call-update) | async-done | bytes 27262992 | tf_op jit(solution)/shard_map/all_gather | solution.py:70
  255.3 71.0 %while.14 = (s32[]{:T(128)}, f32[256,3328]{1,0:T(8,128)}, bf16[8,32,16,256]{3,2,1,0:T(8,128)(2,1)}, bf16[32,8,16,3328]{3,2,1,0:T(8,128)(2,1)}, s32[]{:T(128)}, /*index=5*/s32[]{:T(128)}, s32[]{:T(128)}, s32[]{:T(128)}) while((s32[]{:T(128)}, f32[256,3328]{1,0:T(8,128)}, bf16[8,32,16,256]{3,2,1,0:T(8,128)(2,1)}, ...), condition=%wide.region_2.0_spmd.clone, body=%wide.region_0.0_spmd.clone.sunk | while | flops 883490816 | bytes 30934164 | solution.py:85
  255.3 4.0 %bitcast_convert_fusion.2 = bf16[4,256,3328]{2,1,0:T(8,128)(2,1)S(1)} fusion(bf16[32,8,16,3328]{3,2,1,0:T(8,128)(2,1)} %get-tuple-element.165, s32[]{:T(128)S(6)} %select_n.26, bf16[8,32,16,256]{3,2,1,0:T(8,128)(2,1)} %get-tuple-element.164), kind=kOutput, calls=%fused_computation.clone.1 | convolution fusion | flops 875823104 | bytes 10486784 | tf_op jit(solution)/shard_map/while/body/eval_jaxpr/tgrd,gtrf->gdf/dot_general | solution.py:79
  259.3 1.0 convert_reduce_fusion.2
  260.3 2.1 select_add_fusion.2
  262.4 4.0 %bitcast_convert_fusion.2 = bf16[4,256,3328]{2,1,0:T(8,128)(2,1)S(1)} fusion(bf16[32,8,16,3328]{3,2,1,0:T(8,128)(2,1)} %get-tuple-element.165, s32[]{:T(128)S(6)} %select_n.26, bf16[8,32,16,256]{3,2,1,0:T(8,128)(2,1)} %get-tuple-element.164), kind=kOutput, calls=%fused_computation.clone.1 | convolution fusion | flops 875823104 | bytes 10486784 | tf_op jit(solution)/shard_map/while/body/eval_jaxpr/tgrd,gtrf->gdf/dot_general | solution.py:79
  266.4 1.0 convert_reduce_fusion.2
  267.4 4.1 %select_add_fusion.2 = f32[256,3328]{1,0:T(8,128)} fusion(f32[256,3328]{1,0:T(8,128)S(1)} %convert_reduce_fusion.2, f32[256,3328]{1,0:T(8,128)} %get-tuple-element.155, pred[]{:T(512)S(6)} %compare.3), kind=kLoop, calls=%fused_computation.2.clone.1 | loop fusion | flops 1703936 | bytes 10223617 | tf_op jit(solution)/shard_map/while/body/eval_jaxpr/add | solution.py:83
  271.5 4.0 %bitcast_convert_fusion.2 = bf16[4,256,3328]{2,1,0:T(8,128)(2,1)S(1)} fusion(bf16[32,8,16,3328]{3,2,1,0:T(8,128)(2,1)} %get-tuple-element.165, s32[]{:T(128)S(6)} %select_n.26, bf16[8,32,16,256]{3,2,1,0:T(8,128)(2,1)} %get-tuple-element.164), kind=kOutput, calls=%fused_computation.clone.1 | convolution fusion | flops 875823104 | bytes 10486784 | tf_op jit(solution)/shard_map/while/body/eval_jaxpr/tgrd,gtrf->gdf/dot_general | solution.py:79
  275.6 1.0 convert_reduce_fusion.2
  276.6 4.1 %select_add_fusion.2 = f32[256,3328]{1,0:T(8,128)} fusion(f32[256,3328]{1,0:T(8,128)S(1)} %convert_reduce_fusion.2, f32[256,3328]{1,0:T(8,128)} %get-tuple-element.155, pred[]{:T(512)S(6)} %compare.3), kind=kLoop, calls=%fused_computation.2.clone.1 | loop fusion | flops 1703936 | bytes 10223617 | tf_op jit(solution)/shard_map/while/body/eval_jaxpr/add | solution.py:83
  280.7 4.0 %bitcast_convert_fusion.2 = bf16[4,256,3328]{2,1,0:T(8,128)(2,1)S(1)} fusion(bf16[32,8,16,3328]{3,2,1,0:T(8,128)(2,1)} %get-tuple-element.165, s32[]{:T(128)S(6)} %select_n.26, bf16[8,32,16,256]{3,2,1,0:T(8,128)(2,1)} %get-tuple-element.164), kind=kOutput, calls=%fused_computation.clone.1 | convolution fusion | flops 875823104 | bytes 10486784 | tf_op jit(solution)/shard_map/while/body/eval_jaxpr/tgrd,gtrf->gdf/dot_general | solution.py:79
  284.7 1.0 convert_reduce_fusion.2
  285.7 4.1 %select_add_fusion.2 = f32[256,3328]{1,0:T(8,128)} fusion(f32[256,3328]{1,0:T(8,128)S(1)} %convert_reduce_fusion.2, f32[256,3328]{1,0:T(8,128)} %get-tuple-element.155, pred[]{:T(512)S(6)} %compare.3), kind=kLoop, calls=%fused_computation.2.clone.1 | loop fusion | flops 1703936 | bytes 10223617 | tf_op jit(solution)/shard_map/while/body/eval_jaxpr/add | solution.py:83
  289.8 4.0 %bitcast_convert_fusion.2 = bf16[4,256,3328]{2,1,0:T(8,128)(2,1)S(1)} fusion(bf16[32,8,16,3328]{3,2,1,0:T(8,128)(2,1)} %get-tuple-element.165, s32[]{:T(128)S(6)} %select_n.26, bf16[8,32,16,256]{3,2,1,0:T(8,128)(2,1)} %get-tuple-element.164), kind=kOutput, calls=%fused_computation.clone.1 | convolution fusion | flops 875823104 | bytes 10486784 | tf_op jit(solution)/shard_map/while/body/eval_jaxpr/tgrd,gtrf->gdf/dot_general | solution.py:79
  293.8 1.0 convert_reduce_fusion.2
  294.8 4.1 %select_add_fusion.2 = f32[256,3328]{1,0:T(8,128)} fusion(f32[256,3328]{1,0:T(8,128)S(1)} %convert_reduce_fusion.2, f32[256,3328]{1,0:T(8,128)} %get-tuple-element.155, pred[]{:T(512)S(6)} %compare.3), kind=kLoop, calls=%fused_computation.2.clone.1 | loop fusion | flops 1703936 | bytes 10223617 | tf_op jit(solution)/shard_map/while/body/eval_jaxpr/add | solution.py:83
  298.9 4.0 %bitcast_convert_fusion.2 = bf16[4,256,3328]{2,1,0:T(8,128)(2,1)S(1)} fusion(bf16[32,8,16,3328]{3,2,1,0:T(8,128)(2,1)} %get-tuple-element.165, s32[]{:T(128)S(6)} %select_n.26, bf16[8,32,16,256]{3,2,1,0:T(8,128)(2,1)} %get-tuple-element.164), kind=kOutput, calls=%fused_computation.clone.1 | convolution fusion | flops 875823104 | bytes 10486784 | tf_op jit(solution)/shard_map/while/body/eval_jaxpr/tgrd,gtrf->gdf/dot_general | solution.py:79
  302.9 1.0 convert_reduce_fusion.2
  303.9 4.1 %select_add_fusion.2 = f32[256,3328]{1,0:T(8,128)} fusion(f32[256,3328]{1,0:T(8,128)S(1)} %convert_reduce_fusion.2, f32[256,3328]{1,0:T(8,128)} %get-tuple-element.155, pred[]{:T(512)S(6)} %compare.3), kind=kLoop, calls=%fused_computation.2.clone.1 | loop fusion | flops 1703936 | bytes 10223617 | tf_op jit(solution)/shard_map/while/body/eval_jaxpr/add | solution.py:83
  308.0 4.0 %bitcast_convert_fusion.2 = bf16[4,256,3328]{2,1,0:T(8,128)(2,1)S(1)} fusion(bf16[32,8,16,3328]{3,2,1,0:T(8,128)(2,1)} %get-tuple-element.165, s32[]{:T(128)S(6)} %select_n.26, bf16[8,32,16,256]{3,2,1,0:T(8,128)(2,1)} %get-tuple-element.164), kind=kOutput, calls=%fused_computation.clone.1 | convolution fusion | flops 875823104 | bytes 10486784 | tf_op jit(solution)/shard_map/while/body/eval_jaxpr/tgrd,gtrf->gdf/dot_general | solution.py:79
  312.0 1.0 convert_reduce_fusion.2
  313.1 4.1 %select_add_fusion.2 = f32[256,3328]{1,0:T(8,128)} fusion(f32[256,3328]{1,0:T(8,128)S(1)} %convert_reduce_fusion.2, f32[256,3328]{1,0:T(8,128)} %get-tuple-element.155, pred[]{:T(512)S(6)} %compare.3), kind=kLoop, calls=%fused_computation.2.clone.1 | loop fusion | flops 1703936 | bytes 10223617 | tf_op jit(solution)/shard_map/while/body/eval_jaxpr/add | solution.py:83
  317.1 4.0 %bitcast_convert_fusion.2 = bf16[4,256,3328]{2,1,0:T(8,128)(2,1)S(1)} fusion(bf16[32,8,16,3328]{3,2,1,0:T(8,128)(2,1)} %get-tuple-element.165, s32[]{:T(128)S(6)} %select_n.26, bf16[8,32,16,256]{3,2,1,0:T(8,128)(2,1)} %get-tuple-element.164), kind=kOutput, calls=%fused_computation.clone.1 | convolution fusion | flops 875823104 | bytes 10486784 | tf_op jit(solution)/shard_map/while/body/eval_jaxpr/tgrd,gtrf->gdf/dot_general | solution.py:79
  321.2 1.0 convert_reduce_fusion.2
  322.2 4.1 %select_add_fusion.2 = f32[256,3328]{1,0:T(8,128)} fusion(f32[256,3328]{1,0:T(8,128)S(1)} %convert_reduce_fusion.2, f32[256,3328]{1,0:T(8,128)} %get-tuple-element.155, pred[]{:T(512)S(6)} %compare.3), kind=kLoop, calls=%fused_computation.2.clone.1 | loop fusion | flops 1703936 | bytes 10223617 | tf_op jit(solution)/shard_map/while/body/eval_jaxpr/add | solution.py:83
  326.3 6.5 %subtract_convert_fusion = (bf16[256,3328]{1,0:T(8,128)(2,1)S(1)}, f32[256,3328]{1,0:T(8,128)}) fusion(f32[256,3328]{1,0:T(8,128)} %param.11, f32[]{:T(128)} %bitcast.5, f32[256,3328]{1,0:T(8,128)} %get-tuple-element.81, bf16[256,3328]{1,0:T(8,128)(2,1)} %param.13, f32[]{:T(128)} %bitcast.4, bf16[256,3328]{1,0:T(8,128)(2,1)} %param.12), kind=kLoop, calls=%fused_computation.14 | loop fusion | flops 15335424 | bytes 15335432 | tf_op jit(solution)/shard_map/convert_element_type | solution.py:94
  332.8 4.0 %collective-permute-start = (bf16[256,256]{1,0:T(8,128)(2,1)S(1)}, bf16[256,256]{1,0:T(8,128)(2,1)S(1)}, u32[]{:S(2)}, u32[]{:S(2)}) collective-permute-start(bf16[256,256]{1,0:T(8,128)(2,1)S(1)} %get-tuple-element.120), channel_id=1, source_target_pairs={{0,1},{1,2},{2,3},{3,4},{4,5},{5,6},{6,7},{8,9},{9,10},{10,11},{11... | collective-permute-start | bytes 393224 | tf_op jit(solution)/shard_map/ppermute | solution.py:24
  336.8 1.9 collective-permute-start.1
  338.7 0.6 iota_compare_fusion
  339.4 0.6 dynamic_slice.25
  340.6 0.1 pad_dynamic-slice_fusion.3
  340.7 0.0 collective-permute-done
  340.7 2.4 collective-permute-done.1
  343.1 3.1 fusion.12
  (3 shorter events, 0.0 us)
Async XLA Ops:
  7.2 49.8 %all-gather.3.cloned.1.call-start = ((), (), s32[]{:S(2)}) async-start(), calls=%async_computation.1 | async-start | bytes 2359296 | tf_op jit(solution)/shard_map/all_gather | solution.py:64
  31.3 223.9 %all-gather.5.cloned.1.call-start = ((), (), s32[]{:S(2)}) async-start(), calls=%async_computation.2 | async-start | bytes 28114944 | tf_op jit(solution)/shard_map/all_gather | solution.py:70
  332.8 7.9 %collective-permute-start = (bf16[256,256]{1,0:T(8,128)(2,1)S(1)}, bf16[256,256]{1,0:T(8,128)(2,1)S(1)}, u32[]{:S(2)}, u32[]{:S(2)}) collective-permute-start(bf16[256,256]{1,0:T(8,128)(2,1)S(1)} %get-tuple-element.120), channel_id=1, source_target_pairs={{0,1},{1,2},{2,3},{3,4},{4,5},{5,6},{6,7},{8,9},{9,10},{10,11},{11... | collective-permute-start | bytes 393224 | tf_op jit(solution)/shard_map/ppermute | solution.py:24
  336.8 6.3 %collective-permute-start.1 = (bf16[256,256]{1,0:T(8,128)(2,1)S(1)}, bf16[256,256]{1,0:T(8,128)(2,1)S(1)}, u32[]{:S(2)}, u32[]{:S(2)}) collective-permute-start(bf16[256,256]{1,0:T(8,128)(2,1)S(1)} %get-tuple-element.119), channel_id=1, source_target_pairs={{1,0},{2,1},{3,2},{4,3},{5,4},{6,5},{7,6},{9,8},{10,9},{11,10},{12... | collective-permute-start | bytes 393224 | tf_op jit(solution)/shard_map/ppermute | solution.py:26
Sparse Core Ops, SparseCore 0:
  31.5 25.4 all-gather.2
  59.5 195.6 all-gather.4
where the time goes:
time: 354 us; the launch traced here: 353 us
  waiting for transfers between devices  223 us (63%)
  other arithmetic  50.5 us (14%)
  matrix products  32.1 us (9%)
  blocking collectives  23.1 us (7%)
  between operations  15.5 us (4%)
  starting transfers between devices  6.03 us (2%)
    all_gather x1, waiting for transfers between devices, per_device(): shard_piece = lax.all_gather(hidden, 'dp', axis=0, tiled=True)  198 us
    dot_general x8, matrix products, one_turn(): jnp.einsum('tgrd,gtrf->gdf', grad_block, act_block, preferred_element_typ...  32.1 us
    add x8, other arithmetic, one_turn(): return running + jnp.sum(rounded, axis=0)  30.8 us
    all_to_all x1, blocking collectives, per_device(): lax.all_to_all(out_grad, 'dp', split_axis=1, concat_axis=0, tiled=True)  23.1 us
    all_gather x1, waiting for transfers between devices, per_device(): spread = lax.all_gather(regrouped, 'tensor', axis=0, tiled=True)  21.4 us
    reduce_sum x8, other arithmetic, one_turn(): return running + jnp.sum(rounded, axis=0)  7.96 us
  transfers between devices with their start and end apart: 4, of which 3 were waited for; matrix products, arithmetic and copies ran while one was open for 1% of the time, Pallas kernels for 0%

commit v1 on v0

--- a/solution.py
+++ b/solution.py
@@ -61,7 +61,14 @@
     shard_rows = master.shape[0]
     hidden_units = hidden.shape[1]
     regrouped = lax.all_to_all(out_grad, "dp", split_axis=1, concat_axis=0, tiled=True)
-    spread = lax.all_gather(regrouped, "tensor", axis=0, tiled=True)
+    ring = [regrouped]
+    for hop in range(7):
+        ring.append(lax.ppermute(ring[-1], "tensor", [(dev, (dev + 1) % 8) for dev in range(8)]))
+    spread = jnp.roll(
+        jnp.concatenate(ring[::-1], axis=0),
+        (lax.axis_index("tensor") + 1) * ring[0].shape[0],
+        axis=0,
+    )
     tensor_count = lax.axis_size("tensor")
     data_count = lax.axis_size("dp")
     local_tokens = out_grad.shape[0]

time: 354 us -> 309 us (0.87)
  waiting for transfers between devices: 223 us -> 162 us
  starting transfers between devices: 6.03 us -> 20.3 us
    all_gather x1, waiting for transfers between devices: 198 us -> 131 us  [per_device(): shard_piece = lax.all_gather(hidden, 'dp', axis=0, tiled=True)]
    ppermute x0 -> x7, waiting for transfers between devices: none -> 27.8 us  [per_device(): lax.ppermute(ring[-1], 'tensor', [(dev, (dev + 1) % 8) for dev in range(8)])]
    all_gather x1 -> x0, waiting for transfers between devices: 21.4 us -> none  [per_device(): spread = lax.all_gather(regrouped, 'tensor', axis=0, tiled=True)]
    ppermute x0 -> x7, starting transfers between devices: none -> 14.4 us  [per_device(): lax.ppermute(ring[-1], 'tensor', [(dev, (dev + 1) % 8) for dev in range(8)])]
  transfers between devices with their start and end apart: 4 -> 10, of which waited for: 3 -> 9; matrix products, arithmetic and copies ran while one was open for 1% -> 2% of each run, Pallas kernels for 0% -> 0%
where the time goes in v1:
time: 309 us; the launch traced here: 308 us
  waiting for transfers between devices  162 us (52%)
  other arithmetic  50.5 us (16%)
  matrix products  32.1 us (10%)
  blocking collectives  23 us (7%)
  starting transfers between devices  20.3 us (7%)
  between operations  15.6 us (5%)
  local copies, waits for them, and re-layouts  4.73 us (2%)
    all_gather x1, waiting for transfers between devices, per_device(): shard_piece = lax.all_gather(hidden, 'dp', axis=0, tiled=True)  131 us
    dot_general x8, matrix products, one_turn(): jnp.einsum('tgrd,gtrf->gdf', grad_block, act_block, preferred_element_typ...  32.1 us
    add x8, other arithmetic, one_turn(): return running + jnp.sum(rounded, axis=0)  30.8 us
    ppermute x7, waiting for transfers between devices, per_device(): lax.ppermute(ring[-1], 'tensor', [(dev, (dev + 1) % 8) for dev in range(8)])  27.8 us
    all_to_all x1, blocking collectives, per_device(): lax.all_to_all(out_grad, 'dp', split_axis=1, concat_axis=0, tiled=True)  23 us
    ppermute x7, starting transfers between devices, per_device(): lax.ppermute(ring[-1], 'tensor', [(dev, (dev + 1) % 8) for dev in range(8)])  14.4 us
    reduce_sum x8, other arithmetic, one_turn(): return running + jnp.sum(rounded, axis=0)  7.96 us
    convert_element_type x1, other arithmetic, per_device(): laid = relayout(master_new.astype(jnp.bfloat16), row_counts)  6.5 us
  transfers between devices with their start and end apart: 10, of which 9 were waited for; matrix products, arithmetic and copies ran while one was open for 2% of the time, Pallas kernels for 0%

profile of v1, /device:TPU:1, one launch (start us, length us, event | category | flops | bytes accessed | tf_op | source)
XLA Modules:
  0.0 308.0 jit_solution(4666907586323091156)
XLA Ops:
  7.9 1.0 copy.20
  8.9 23.0 %all_to_all.19 = bf16[16,32,256]{2,0,1:T(8,128)(2,1)S(1)} all-to-all(bf16[16,32,256]{2,0,1:T(8,128)(2,1)S(1)} %bitcast.24), channel_id=1, replica_groups=mesh['dp'=32,'tensor'=8] {'dp'}, dimensions={1} | all-to-all | bytes 524288 | tf_op jit(solution)/shard_map/all_to_all | solution.py:63
  31.9 3.7 %collective-permute-start = (bf16[512,256]{1,0:T(8,128)(2,1)S(1)}, bf16[512,256]{1,0:T(8,128)(2,1)S(1)}, u32[]{:S(2)}, u32[]{:S(2)}) collective-permute-start(bf16[512,256]{1,0:T(8,128)(2,1)S(1)} %bitcast.21), channel_id=1, source_target_pairs={{0,1},{1,2},{2,3},{3,4},{4,5},{5,6},{6,7},{7,0},{8,9},{9,10},{10,1... | collective-permute-start | bytes 786440 | tf_op jit(solution)/shard_map/ppermute | solution.py:66
  35.5 3.3 %collective-permute-done = bf16[512,256]{1,0:T(8,128)(2,1)S(1)} collective-permute-done((bf16[512,256]{1,0:T(8,128)(2,1)S(1)}, bf16[512,256]{1,0:T(8,128)(2,1)S(1)}, u32[]{:S(2)}, u32[]{:S(2)}) %collective-permute-start) | collective-permute-done | bytes 262176 | tf_op jit(solution)/shard_map/ppermute | solution.py:66
  38.9 2.5 collective-permute-start.1
  41.3 3.3 %collective-permute-done.1 = bf16[512,256]{1,0:T(8,128)(2,1)S(1)} collective-permute-done((bf16[512,256]{1,0:T(8,128)(2,1)S(1)}, bf16[512,256]{1,0:T(8,128)(2,1)S(1)}, u32[]{:S(2)}, u32[]{:S(2)}) %collective-permute-start.1) | collective-permute-done | bytes 262176 | tf_op jit(solution)/shard_map/ppermute | solution.py:66
  44.7 2.5 collective-permute-start.2
  47.1 3.3 %collective-permute-done.2 = bf16[512,256]{1,0:T(8,128)(2,1)S(1)} collective-permute-done((bf16[512,256]{1,0:T(8,128)(2,1)S(1)}, bf16[512,256]{1,0:T(8,128)(2,1)S(1)}, u32[]{:S(2)}, u32[]{:S(2)}) %collective-permute-start.2) | collective-permute-done | bytes 262176 | tf_op jit(solution)/shard_map/ppermute | solution.py:66
  50.5 2.5 collective-permute-start.3
  52.9 3.6 %collective-permute-done.3 = bf16[512,256]{1,0:T(8,128)(2,1)S(1)} collective-permute-done((bf16[512,256]{1,0:T(8,128)(2,1)S(1)}, bf16[512,256]{1,0:T(8,128)(2,1)S(1)}, u32[]{:S(2)}, u32[]{:S(2)}) %collective-permute-start.3) | collective-permute-done | bytes 262176 | tf_op jit(solution)/shard_map/ppermute | solution.py:66
  56.5 2.2 collective-permute-start.4
  58.7 4.8 %collective-permute-done.4 = bf16[512,256]{1,0:T(8,128)(2,1)S(1)} collective-permute-done((bf16[512,256]{1,0:T(8,128)(2,1)S(1)}, bf16[512,256]{1,0:T(8,128)(2,1)S(1)}, u32[]{:S(2)}, u32[]{:S(2)}) %collective-permute-start.4) | collective-permute-done | bytes 262176 | tf_op jit(solution)/shard_map/ppermute | solution.py:66
  63.5 1.0 collective-permute-start.5
  64.5 6.0 %collective-permute-done.5 = bf16[512,256]{1,0:T(8,128)(2,1)S(1)} collective-permute-done((bf16[512,256]{1,0:T(8,128)(2,1)S(1)}, bf16[512,256]{1,0:T(8,128)(2,1)S(1)}, u32[]{:S(2)}, u32[]{:S(2)}) %collective-permute-start.5) | collective-permute-done | bytes 262176 | tf_op jit(solution)/shard_map/ppermute | solution.py:66
  72.1 1.3 dynamic_slice.29
  74.0 3.5 %collective-permute-done.6 = bf16[512,256]{1,0:T(8,128)(2,1)S(1)} collective-permute-done((bf16[512,256]{1,0:T(8,128)(2,1)S(1)}, bf16[512,256]{1,0:T(8,128)(2,1)S(1)}, u32[]{:S(2)}, u32[]{:S(2)}) %collective-permute-start.6) | collective-permute-done | bytes 262176 | tf_op jit(solution)/shard_map/ppermute | solution.py:66
  78.0 1.5 constant_dynamic-slice_fusion.1
  79.4 130.7 %all-gather.2.cloned.1.call-done = bf16[4096,3328]{1,0:T(8,128)(2,1)} async-done(((bf16[128,3328]{1,0:T(8,128)(2,1)}), bf16[4096,3328]{1,0:T(8,128)(2,1)}) %all-gather.2.cloned.1.call-update) | async-done | bytes 27262992 | tf_op jit(solution)/shard_map/all_gather | solution.py:77
  210.2 71.0 %while.14 = (s32[]{:T(128)}, f32[256,3328]{1,0:T(8,128)}, bf16[8,32,16,256]{3,2,1,0:T(8,128)(2,1)}, bf16[32,8,16,3328]{3,2,1,0:T(8,128)(2,1)}, s32[]{:T(128)}, /*index=5*/s32[]{:T(128)}, s32[]{:T(128)}, s32[]{:T(128)}) while((s32[]{:T(128)}, f32[256,3328]{1,0:T(8,128)}, bf16[8,32,16,256]{3,2,1,0:T(8,128)(2,1)}, ...), condition=%wide.region_2.3_spmd.clone, body=%wide.region_0.2_spmd.clone.sunk | while | flops 883490816 | bytes 30934156 | solution.py:92
  210.2 4.0 %bitcast_convert_fusion.2 = bf16[4,256,3328]{2,1,0:T(8,128)(2,1)S(1)} fusion(bf16[32,8,16,3328]{3,2,1,0:T(8,128)(2,1)} %get-tuple-element.165, s32[]{:T(128)S(6)} %select_n.41, bf16[8,32,16,256]{3,2,1,0:T(8,128)(2,1)} %get-tuple-element.164), kind=kOutput, calls=%fused_computation.clone.1 | convolution fusion | flops 875823104 | bytes 10486784 | tf_op jit(solution)/shard_map/while/body/eval_jaxpr/tgrd,gtrf->gdf/dot_general | solution.py:86
  214.2 1.0 convert_reduce_fusion.2
  215.2 2.1 select_add_fusion.2
  217.3 4.0 %bitcast_convert_fusion.2 = bf16[4,256,3328]{2,1,0:T(8,128)(2,1)S(1)} fusion(bf16[32,8,16,3328]{3,2,1,0:T(8,128)(2,1)} %get-tuple-element.165, s32[]{:T(128)S(6)} %select_n.41, bf16[8,32,16,256]{3,2,1,0:T(8,128)(2,1)} %get-tuple-element.164), kind=kOutput, calls=%fused_computation.clone.1 | convolution fusion | flops 875823104 | bytes 10486784 | tf_op jit(solution)/shard_map/while/body/eval_jaxpr/tgrd,gtrf->gdf/dot_general | solution.py:86
  221.4 1.0 convert_reduce_fusion.2
  222.4 4.1 %select_add_fusion.2 = f32[256,3328]{1,0:T(8,128)} fusion(f32[256,3328]{1,0:T(8,128)S(1)} %convert_reduce_fusion.2, f32[256,3328]{1,0:T(8,128)} %get-tuple-element.155, pred[]{:T(512)S(6)} %compare.4), kind=kLoop, calls=%fused_computation.2.clone.1 | loop fusion | flops 1703936 | bytes 10223617 | tf_op jit(solution)/shard_map/while/body/eval_jaxpr/add | solution.py:90
  226.5 4.0 %bitcast_convert_fusion.2 = bf16[4,256,3328]{2,1,0:T(8,128)(2,1)S(1)} fusion(bf16[32,8,16,3328]{3,2,1,0:T(8,128)(2,1)} %get-tuple-element.165, s32[]{:T(128)S(6)} %select_n.41, bf16[8,32,16,256]{3,2,1,0:T(8,128)(2,1)} %get-tuple-element.164), kind=kOutput, calls=%fused_computation.clone.1 | convolution fusion | flops 875823104 | bytes 10486784 | tf_op jit(solution)/shard_map/while/body/eval_jaxpr/tgrd,gtrf->gdf/dot_general | solution.py:86
  230.5 1.0 convert_reduce_fusion.2
  231.5 4.1 %select_add_fusion.2 = f32[256,3328]{1,0:T(8,128)} fusion(f32[256,3328]{1,0:T(8,128)S(1)} %convert_reduce_fusion.2, f32[256,3328]{1,0:T(8,128)} %get-tuple-element.155, pred[]{:T(512)S(6)} %compare.4), kind=kLoop, calls=%fused_computation.2.clone.1 | loop fusion | flops 1703936 | bytes 10223617 | tf_op jit(solution)/shard_map/while/body/eval_jaxpr/add | solution.py:90
  235.6 4.0 %bitcast_convert_fusion.2 = bf16[4,256,3328]{2,1,0:T(8,128)(2,1)S(1)} fusion(bf16[32,8,16,3328]{3,2,1,0:T(8,128)(2,1)} %get-tuple-element.165, s32[]{:T(128)S(6)} %select_n.41, bf16[8,32,16,256]{3,2,1,0:T(8,128)(2,1)} %get-tuple-element.164), kind=kOutput, calls=%fused_computation.clone.1 | convolution fusion | flops 875823104 | bytes 10486784 | tf_op jit(solution)/shard_map/while/body/eval_jaxpr/tgrd,gtrf->gdf/dot_general | solution.py:86
  239.6 1.0 convert_reduce_fusion.2
  240.6 4.1 %select_add_fusion.2 = f32[256,3328]{1,0:T(8,128)} fusion(f32[256,3328]{1,0:T(8,128)S(1)} %convert_reduce_fusion.2, f32[256,3328]{1,0:T(8,128)} %get-tuple-element.155, pred[]{:T(512)S(6)} %compare.4), kind=kLoop, calls=%fused_computation.2.clone.1 | loop fusion | flops 1703936 | bytes 10223617 | tf_op jit(solution)/shard_map/while/body/eval_jaxpr/add | solution.py:90
  244.7 4.0 %bitcast_convert_fusion.2 = bf16[4,256,3328]{2,1,0:T(8,128)(2,1)S(1)} fusion(bf16[32,8,16,3328]{3,2,1,0:T(8,128)(2,1)} %get-tuple-element.165, s32[]{:T(128)S(6)} %select_n.41, bf16[8,32,16,256]{3,2,1,0:T(8,128)(2,1)} %get-tuple-element.164), kind=kOutput, calls=%fused_computation.clone.1 | convolution fusion | flops 875823104 | bytes 10486784 | tf_op jit(solution)/shard_map/while/body/eval_jaxpr/tgrd,gtrf->gdf/dot_general | solution.py:86
  248.7 1.0 convert_reduce_fusion.2
  249.7 4.1 %select_add_fusion.2 = f32[256,3328]{1,0:T(8,128)} fusion(f32[256,3328]{1,0:T(8,128)S(1)} %convert_reduce_fusion.2, f32[256,3328]{1,0:T(8,128)} %get-tuple-element.155, pred[]{:T(512)S(6)} %compare.4), kind=kLoop, calls=%fused_computation.2.clone.1 | loop fusion | flops 1703936 | bytes 10223617 | tf_op jit(solution)/shard_map/while/body/eval_jaxpr/add | solution.py:90
  253.8 4.0 %bitcast_convert_fusion.2 = bf16[4,256,3328]{2,1,0:T(8,128)(2,1)S(1)} fusion(bf16[32,8,16,3328]{3,2,1,0:T(8,128)(2,1)} %get-tuple-element.165, s32[]{:T(128)S(6)} %select_n.41, bf16[8,32,16,256]{3,2,1,0:T(8,128)(2,1)} %get-tuple-element.164), kind=kOutput, calls=%fused_computation.clone.1 | convolution fusion | flops 875823104 | bytes 10486784 | tf_op jit(solution)/shard_map/while/body/eval_jaxpr/tgrd,gtrf->gdf/dot_general | solution.py:86
  257.9 1.0 convert_reduce_fusion.2
  258.9 4.1 %select_add_fusion.2 = f32[256,3328]{1,0:T(8,128)} fusion(f32[256,3328]{1,0:T(8,128)S(1)} %convert_reduce_fusion.2, f32[256,3328]{1,0:T(8,128)} %get-tuple-element.155, pred[]{:T(512)S(6)} %compare.4), kind=kLoop, calls=%fused_computation.2.clone.1 | loop fusion | flops 1703936 | bytes 10223617 | tf_op jit(solution)/shard_map/while/body/eval_jaxpr/add | solution.py:90
  263.0 4.0 %bitcast_convert_fusion.2 = bf16[4,256,3328]{2,1,0:T(8,128)(2,1)S(1)} fusion(bf16[32,8,16,3328]{3,2,1,0:T(8,128)(2,1)} %get-tuple-element.165, s32[]{:T(128)S(6)} %select_n.41, bf16[8,32,16,256]{3,2,1,0:T(8,128)(2,1)} %get-tuple-element.164), kind=kOutput, calls=%fused_computation.clone.1 | convolution fusion | flops 875823104 | bytes 10486784 | tf_op jit(solution)/shard_map/while/body/eval_jaxpr/tgrd,gtrf->gdf/dot_general | solution.py:86
  267.0 1.0 convert_reduce_fusion.2
  268.0 4.1 %select_add_fusion.2 = f32[256,3328]{1,0:T(8,128)} fusion(f32[256,3328]{1,0:T(8,128)S(1)} %convert_reduce_fusion.2, f32[256,3328]{1,0:T(8,128)} %get-tuple-element.155, pred[]{:T(512)S(6)} %compare.4), kind=kLoop, calls=%fused_computation.2.clone.1 | loop fusion | flops 1703936 | bytes 10223617 | tf_op jit(solution)/shard_map/while/body/eval_jaxpr/add | solution.py:90
  272.1 4.0 %bitcast_convert_fusion.2 = bf16[4,256,3328]{2,1,0:T(8,128)(2,1)S(1)} fusion(bf16[32,8,16,3328]{3,2,1,0:T(8,128)(2,1)} %get-tuple-element.165, s32[]{:T(128)S(6)} %select_n.41, bf16[8,32,16,256]{3,2,1,0:T(8,128)(2,1)} %get-tuple-element.164), kind=kOutput, calls=%fused_computation.clone.1 | convolution fusion | flops 875823104 | bytes 10486784 | tf_op jit(solution)/shard_map/while/body/eval_jaxpr/tgrd,gtrf->gdf/dot_general | solution.py:86
  276.1 1.0 convert_reduce_fusion.2
  277.1 4.1 %select_add_fusion.2 = f32[256,3328]{1,0:T(8,128)} fusion(f32[256,3328]{1,0:T(8,128)S(1)} %convert_reduce_fusion.2, f32[256,3328]{1,0:T(8,128)} %get-tuple-element.155, pred[]{:T(512)S(6)} %compare.4), kind=kLoop, calls=%fused_computation.2.clone.1 | loop fusion | flops 1703936 | bytes 10223617 | tf_op jit(solution)/shard_map/while/body/eval_jaxpr/add | solution.py:90
  281.2 6.5 %subtract_convert_fusion = (bf16[256,3328]{1,0:T(8,128)(2,1)S(1)}, f32[256,3328]{1,0:T(8,128)}) fusion(f32[256,3328]{1,0:T(8,128)} %param.11, f32[]{:T(128)} %bitcast.5, f32[256,3328]{1,0:T(8,128)} %get-tuple-element.81, bf16[256,3328]{1,0:T(8,128)(2,1)} %param.13, f32[]{:T(128)} %bitcast.4, bf16[256,3328]{1,0:T(8,128)(2,1)} %param.12), kind=kLoop, calls=%fused_computation.14 | loop fusion | flops 15335424 | bytes 15335432 | tf_op jit(solution)/shard_map/convert_element_type | solution.py:101
  287.7 4.0 %collective-permute-start.7 = (bf16[256,256]{1,0:T(8,128)(2,1)S(1)}, bf16[256,256]{1,0:T(8,128)(2,1)S(1)}, u32[]{:S(2)}, u32[]{:S(2)}) collective-permute-start(bf16[256,256]{1,0:T(8,128)(2,1)S(1)} %get-tuple-element.120), channel_id=1, source_target_pairs={{0,1},{1,2},{2,3},{3,4},{4,5},{5,6},{6,7},{8,9},{9,10},{10,11},{11... | collective-permute-start | bytes 393224 | tf_op jit(solution)/shard_map/ppermute | solution.py:24
  291.8 1.9 collective-permute-start.8
  295.7 2.4 collective-permute-done.8
  298.0 3.1 %fusion.12 = bf16[256,3840]{1,0:T(8,128)(2,1)} fusion(s32[]{:T(128)S(6)} %select_n.36, bf16[256,256]{1,0:T(8,128)(2,1)S(1)} %collective-permute-done.7, bf16[256,3328]{1,0:T(8,128)(2,1)S(1)} %get-tuple-element.117, bf16[256,256]{1,0:T(8,128)(2,1)S(1)} %collective-permute-done.8, pred[3840]{0:T(1024)(128)(4,1)S(1)} %iota_compare_fusion, ...), kind=kLoop, calls=%fused_computation.22 | loop fusion | flops 8847360 | bytes 3943684 | tf_op jit(solution)/shard_map/jit(_where)/select_n | solution.py:57
  (28 shorter events, 3.9 us)
Async XLA Ops:
  7.2 203.0 %all-gather.2.cloned.1.call-start = ((), (), s32[]{:S(2)}) async-start(), calls=%async_computation.1 | async-start | bytes 28114944 | tf_op jit(solution)/shard_map/all_gather | solution.py:77
  31.9 7.0 %collective-permute-start = (bf16[512,256]{1,0:T(8,128)(2,1)S(1)}, bf16[512,256]{1,0:T(8,128)(2,1)S(1)}, u32[]{:S(2)}, u32[]{:S(2)}) collective-permute-start(bf16[512,256]{1,0:T(8,128)(2,1)S(1)} %bitcast.21), channel_id=1, source_target_pairs={{0,1},{1,2},{2,3},{3,4},{4,5},{5,6},{6,7},{7,0},{8,9},{9,10},{10,1... | collective-permute-start | bytes 786440 | tf_op jit(solution)/shard_map/ppermute | solution.py:66
  38.9 5.8 %collective-permute-start.1 = (bf16[512,256]{1,0:T(8,128)(2,1)S(1)}, bf16[512,256]{1,0:T(8,128)(2,1)S(1)}, u32[]{:S(2)}, u32[]{:S(2)}) collective-permute-start(bf16[512,256]{1,0:T(8,128)(2,1)S(1)} %collective-permute-done), channel_id=1, source_target_pairs={{0,1},{1,2},{2,3},{3,4},{4,5},{5,6},{6,7},{7,0},{8,9},{9,10},{10,1... | collective-permute-start | bytes 786440 | tf_op jit(solution)/shard_map/ppermute | solution.py:66
  44.7 5.8 %collective-permute-start.2 = (bf16[512,256]{1,0:T(8,128)(2,1)S(1)}, bf16[512,256]{1,0:T(8,128)(2,1)S(1)}, u32[]{:S(2)}, u32[]{:S(2)}) collective-permute-start(bf16[512,256]{1,0:T(8,128)(2,1)S(1)} %collective-permute-done.1), channel_id=1, source_target_pairs={{0,1},{1,2},{2,3},{3,4},{4,5},{5,6},{6,7},{7,0},{8,9},{9,10},{10,1... | collective-permute-start | bytes 786440 | tf_op jit(solution)/shard_map/ppermute | solution.py:66
  50.5 6.0 %collective-permute-start.3 = (bf16[512,256]{1,0:T(8,128)(2,1)S(1)}, bf16[512,256]{1,0:T(8,128)(2,1)S(1)}, u32[]{:S(2)}, u32[]{:S(2)}) collective-permute-start(bf16[512,256]{1,0:T(8,128)(2,1)S(1)} %collective-permute-done.2), channel_id=1, source_target_pairs={{0,1},{1,2},{2,3},{3,4},{4,5},{5,6},{6,7},{7,0},{8,9},{9,10},{10,1... | collective-permute-start | bytes 786440 | tf_op jit(solution)/shard_map/ppermute | solution.py:66
  56.5 7.0 %collective-permute-start.4 = (bf16[512,256]{1,0:T(8,128)(2,1)S(1)}, bf16[512,256]{1,0:T(8,128)(2,1)S(1)}, u32[]{:S(2)}, u32[]{:S(2)}) collective-permute-start(bf16[512,256]{1,0:T(8,128)(2,1)S(1)} %collective-permute-done.3), channel_id=1, source_target_pairs={{0,1},{1,2},{2,3},{3,4},{4,5},{5,6},{6,7},{7,0},{8,9},{9,10},{10,1... | collective-permute-start | bytes 786440 | tf_op jit(solution)/shard_map/ppermute | solution.py:66
  63.5 7.0 %collective-permute-start.5 = (bf16[512,256]{1,0:T(8,128)(2,1)S(1)}, bf16[512,256]{1,0:T(8,128)(2,1)S(1)}, u32[]{:S(2)}, u32[]{:S(2)}) collective-permute-start(bf16[512,256]{1,0:T(8,128)(2,1)S(1)} %collective-permute-done.4), channel_id=1, source_target_pairs={{0,1},{1,2},{2,3},{3,4},{4,5},{5,6},{6,7},{7,0},{8,9},{9,10},{10,1... | collective-permute-start | bytes 786440 | tf_op jit(solution)/shard_map/ppermute | solution.py:66
  70.5 7.0 %collective-permute-start.6 = (bf16[512,256]{1,0:T(8,128)(2,1)S(1)}, bf16[512,256]{1,0:T(8,128)(2,1)S(1)}, u32[]{:S(2)}, u32[]{:S(2)}) collective-permute-start(bf16[512,256]{1,0:T(8,128)(2,1)S(1)} %collective-permute-done.5), channel_id=1, source_target_pairs={{0,1},{1,2},{2,3},{3,4},{4,5},{5,6},{6,7},{7,0},{8,9},{9,10},{10,1... | collective-permute-start | bytes 786440 | tf_op jit(solution)/shard_map/ppermute | solution.py:66
  287.7 8.0 %collective-permute-start.7 = (bf16[256,256]{1,0:T(8,128)(2,1)S(1)}, bf16[256,256]{1,0:T(8,128)(2,1)S(1)}, u32[]{:S(2)}, u32[]{:S(2)}) collective-permute-start(bf16[256,256]{1,0:T(8,128)(2,1)S(1)} %get-tuple-element.120), channel_id=1, source_target_pairs={{0,1},{1,2},{2,3},{3,4},{4,5},{5,6},{6,7},{8,9},{9,10},{10,11},{11... | collective-permute-start | bytes 393224 | tf_op jit(solution)/shard_map/ppermute | solution.py:24
  291.8 6.3 %collective-permute-start.8 = (bf16[256,256]{1,0:T(8,128)(2,1)S(1)}, bf16[256,256]{1,0:T(8,128)(2,1)S(1)}, u32[]{:S(2)}, u32[]{:S(2)}) collective-permute-start(bf16[256,256]{1,0:T(8,128)(2,1)S(1)} %get-tuple-element.119), channel_id=1, source_target_pairs={{1,0},{2,1},{3,2},{4,3},{5,4},{6,5},{7,6},{9,8},{10,9},{11,10},{12... | collective-permute-start | bytes 393224 | tf_op jit(solution)/shard_map/ppermute | solution.py:26
Sparse Core Ops, SparseCore 0:
  10.6 199.5 all-gather.1
